TPU v7x, 32 devices: a whole 2x2x4 slice. The times are simulated.
32 devices in a mesh: groups: 2 (over y), sec: 2 (over x), row: 4 (over z), col: 2 (over core).
Axes of the slice: x: 2, y: 2, z: 4, core: 2. Of those that a mesh axis runs over, the one named last changes fastest.
Arguments:
- factors: bfloat16 [4, 2048, 2048], P(('groups', 'sec'), 'row', 'col'), parts along dimension 0, may hold values from -0.125 to 0.125
- inverses: bfloat16 [4, 2048, 2048], P(('groups', 'sec'), 'row', 'col'), parts along dimension 0, may hold values from -1.4 to 1.4, as said below
- sigma_end: float32 [4096, 2048], P(('groups', 'row'), 'col'), parts along dimension 0, may hold values from -1 to 6, as said below
Outputs:
- variance: float32 [4, 2048, 2048], P(('groups', 'sec'), 'row', 'col'), parts along dimension 0
There are 2 independent parts, one for each index of `groups`. A program takes and returns all parts, laid end to end along the dimension named above; each array names one. Nothing has to cross between parts.
Inputs may be any that keep to these rules, and one draw needn't show every extreme that they name: inverses[t] is lower triangular; its diagonal entries lie in 0.6 to 1.4. sigma_end is symmetric with diagonal entries in 2.5 to 6.
All inputs are finite; a program needn't handle non-finite values.
Results may differ from a plain program's by a relative error of at most 0.011.
Values may be sent and summed in bfloat16 or wider, within the bound.
A program may use at most 64 MiB of HBM per device.

v0:
```python
import jax
import jax.numpy as jnp
from jax import lax
from jax.sharding import PartitionSpec as P


def partner(shard, axis, stride):
    return lax.ppermute(shard, axis, [(i, i ^ 1 << stride) for i in range(lax.axis_size(axis))])


def passed_along(value, axis, steps):
    count = lax.axis_size(axis)
    first, last = (max(0, -steps), min(count, count - steps))
    return lax.ppermute(value, axis, [(source, source + steps) for source in range(first, last)])


def local(factors, inverses, sigma_end):
    row_size = lax.axis_size("row")
    col_size = lax.axis_size("col")
    sec_size = lax.axis_size("sec")
    row_index = lax.axis_index("row")
    col_index = lax.axis_index("col")
    sec_index = lax.axis_index("sec")
    step_count, tile_rows, tile_cols = factors.shape
    per_column = row_size // col_size
    offset = row_index % per_column * tile_rows
    owner = row_index // per_column
    owns_panel = col_index == owner

    def own_columns(full_panel):
        return lax.dynamic_slice_in_dim(full_panel, offset, tile_rows, 2)

    factor_full, inverse_full = (
        lax.all_gather(factors, "row", axis=1, tiled=True),
        lax.all_gather(inverses, "row", axis=1, tiled=True),
    )
    local_pair = (own_columns(factor_full), own_columns(inverse_full))
    partner_pair = partner((local_pair[0], local_pair[1]), "col", 0)
    factor_left = jnp.where(owns_panel, local_pair[0], partner_pair[0])
    inverse_left = jnp.where(owns_panel, local_pair[1], partner_pair[1])
    diagonal = jnp.einsum(
        "skr,skc->src", inverse_left, inverse_full, preferred_element_type=jnp.float32
    )
    end_low = sigma_end.astype(jnp.bfloat16)

    def run_segment(segment_number, carried):
        state_low, results = carried
        shifted = passed_along(state_low, "sec", -1)
        current = jnp.where(sec_index == sec_size - 1, end_low, shifted)
        active = sec_index == sec_size - 1 - segment_number
        produced = [None] * step_count
        state_full = lax.all_gather(current, "col", axis=1, tiled=True)
        image = jnp.dot(state_full, factor_full[0], preferred_element_type=jnp.float32).astype(
            jnp.bfloat16
        )
        left_panel = factor_left[0]

        def accumulate(running, incoming_rows, first_row, left_panel=left_panel):
            return running + lax.dot_general(
                left_panel,
                incoming_rows,
                (((0,), (0,)), ((), ())),
                preferred_element_type=jnp.float32,
            )

        variance_block = accumulate(
            diagonal[0], lax.all_gather(image, "row", axis=0, tiled=True), jnp.int32(0)
        )
        produced[0] = variance_block
        current = variance_block.astype(jnp.bfloat16)
        results = jnp.where(active, jnp.stack(produced), results)
        return (current, results)

    initial = (end_low, jnp.zeros((step_count, tile_rows, tile_cols), jnp.float32))
    finished = lax.fori_loop(0, sec_size, run_segment, initial)
    return finished[1]


def solution(mesh):
    in_specs = (
        P(("groups", "sec"), "row", "col"),
        P(("groups", "sec"), "row", "col"),
        P(("groups", "row"), "col"),
    )
    out_specs = P(("groups", "sec"), "row", "col")
    return jax.shard_map(local, mesh=mesh, in_specs=in_specs, out_specs=out_specs, check_vma=False)
```

profile of v0, /device:TPU:1, one launch (start us, length us, event | category | flops | bytes accessed | tf_op | source)
XLA Modules:
  0.0 458.8 jit_solution(6147883923048715536)
XLA Ops:
  6.5 0.0 all-gather.5.cloned.1.call-start
  6.5 0.7 all-gather.5.cloned.1.call-update
  7.3 0.0 all-gather.7.cloned.1.call-start
  7.3 0.7 all-gather.7.cloned.1.call-update
  8.0 83.8 %all-gather.5.cloned.1.call-done = bf16[1,2048,1024]{2,1,0:T(8,128)(2,1)} async-done(((bf16[1,512,1024]{2,1,0:T(8,128)(2,1)}), bf16[1,2048,1024]{2,1,0:T(8,128)(2,1)}) %all-gather.5.cloned.1.call-update) | async-done | bytes 4194320 | tf_op jit(solution)/shard_map/all_gather | solution.py:35
  91.8 3.0 constant_dynamic-slice_fusion.1
  94.9 0.7 collective-permute-start.1
  95.5 77.2 %all-gather.7.cloned.1.call-done = bf16[1,2048,1024]{2,1,0:T(8,128)(2,1)} async-done(((bf16[1,512,1024]{2,1,0:T(8,128)(2,1)}), bf16[1,2048,1024]{2,1,0:T(8,128)(2,1)}) %all-gather.7.cloned.1.call-update) | async-done | bytes 4194320 | tf_op jit(solution)/shard_map/all_gather | solution.py:34
  172.7 3.1 constant_dynamic-slice_fusion
  175.8 0.7 collective-permute-start.2
  176.5 1.8 copy.4
  178.2 0.0 copy-start
  178.2 0.0 copy-start.2
  178.3 0.0 collective-permute-done.1
  178.3 7.0 %fusion.14 = f32[1,512,1024]{1,2,0:T(8,128)} fusion(bf16[1,2048,1024]{2,1,0:T(8,128)(2,1)} %all-gather.5.cloned.1.call-done, bf16[1,2048,512]{2,1,0:T(8,128)(2,1)} %constant_dynamic-slice_fusion.1, bf16[1,2048,512]{2,1,0:T(8,128)(2,1)} %collective-permute-done.1, pred[]{:T(512)S(6)} %eq.22), kind=kOutput, calls=%fused_computation.14 | convolution fusion | flops 2148532224 | bytes 10485761 | tf_op jit(solution)/shard_map/skr,skc->src/dot_general | solution.py:41
  185.3 0.0 copy-done
  185.3 0.0 collective-permute-done.2
  185.3 0.0 copy-done.2
  185.3 0.0 copy-start.1
  185.3 3.9 broadcast_select_fusion.1
  189.2 0.0 copy-done.1
  189.2 261.0 %while.17 = (s32[]{:T(128)}, bf16[512,1024]{0,1:T(8,128)(2,1)S(1)}, f32[1,512,1024]{1,2,0:T(8,128)S(1)}, f32[1,512,1024]{1,2,0:T(8,128)}, pred[]{:T(512)}, /*ind...) while((s32[]{:T(128)}, bf16[512,1024]{0,1:T(8,128)(2,1)S(1)}, ...), condition=%wide.region_1.2_spmd.clone, body=%wide.region_0.1_spmd.clone.sunk | while | flops 4298113024 | bytes 57671944 | solution.py:75
  189.2 0.0 all-gather.9.cloned.1.call-start
  189.2 1.3 collective-permute-start
  190.4 24.3 %collective-permute-done = bf16[512,1024]{0,1:T(8,128)(2,1)S(1)} collective-permute-done((bf16[512,1024]{0,1:T(8,128)(2,1)S(1)}, bf16[512,1024]{0,1:T(8,128)(2,1)S(1)}, u32[]{:S(2)}, u32[]{:S(2)}) %collective-permute-start) | collective-permute-done | bytes 1048608 | tf_op jit(solution)/shard_map/while/body/eval_jaxpr/ppermute | solution.py:14
  214.7 1.1 broadcast_select_fusion.3
  215.8 0.0 all-gather.9.cloned.1.call-update
  215.8 0.0 all-gather.11.cloned.1.call-start
  215.9 8.4 %all-gather.9.cloned.1.call-done = bf16[512,2048]{0,1:T(8,128)(2,1)} async-done(((bf16[512,1024]{0,1:T(8,128)(2,1)}), bf16[512,2048]{0,1:T(8,128)(2,1)}) %all-gather.9.cloned.1.call-update) | async-done | bytes 2097168 | tf_op jit(solution)/shard_map/while/body/eval_jaxpr/all_gather | solution.py:52
  224.3 6.1 %fusion.30 = bf16[512,1024]{1,0:T(8,128)(2,1)} fusion(bf16[512,2048]{0,1:T(8,128)(2,1)} %all-gather.9.cloned.1.call-done, bf16[1,2048,1024]{2,1,0:T(8,128)(2,1)} %get-tuple-element.328), kind=kOutput, calls=%fused_computation.6.clone.1 | convolution fusion | flops 2148007936 | bytes 7340032 | tf_op jit(solution)/shard_map/while/body/eval_jaxpr/dot_general | solution.py:53
  230.4 0.0 all-gather.11.cloned.1.call-update
  230.5 81.7 %all-gather.11.cloned.1.call-done = bf16[2048,1024]{1,0:T(8,128)(2,1)} async-done(((bf16[512,1024]{1,0:T(8,128)(2,1)}), bf16[2048,1024]{1,0:T(8,128)(2,1)}) %all-gather.11.cloned.1.call-update) | async-done | bytes 4194320 | tf_op jit(solution)/shard_map/while/body/eval_jaxpr/all_gather | solution.py:67
  312.2 5.8 %fusion.31 = (bf16[512,1024]{0,1:T(8,128)(2,1)S(1)}, f32[512,1024]{0,1:T(8,128)S(1)}) fusion(bf16[2048,1024]{1,0:T(8,128)(2,1)} %all-gather.11.cloned.1.call-done, bf16[1,2048,512]{2,1,0:T(8,128)(2,1)} %get-tuple-element.329, f32[1,512,1024]{1,2,0:T(8,128)} %get-tuple-element.325), kind=kOutput, calls=%fused_computation.17.clone.1 | convolution fusion | flops 2148532224 | bytes 11534336 | tf_op jit(solution)/shard_map/while/body/eval_jaxpr/dot_general | solution.py:59
  318.0 0.7 bitcast_select_fusion.2
  318.7 0.0 all-gather.9.cloned.1.call-start
  318.8 1.3 collective-permute-start
  320.1 24.6 %collective-permute-done = bf16[512,1024]{0,1:T(8,128)(2,1)S(1)} collective-permute-done((bf16[512,1024]{0,1:T(8,128)(2,1)S(1)}, bf16[512,1024]{0,1:T(8,128)(2,1)S(1)}, u32[]{:S(2)}, u32[]{:S(2)}) %collective-permute-start) | collective-permute-done | bytes 1048608 | tf_op jit(solution)/shard_map/while/body/eval_jaxpr/ppermute | solution.py:14
  344.7 1.1 broadcast_select_fusion.3
  345.8 0.0 all-gather.9.cloned.1.call-update
  345.8 0.0 all-gather.11.cloned.1.call-start
  345.9 9.9 %all-gather.9.cloned.1.call-done = bf16[512,2048]{0,1:T(8,128)(2,1)} async-done(((bf16[512,1024]{0,1:T(8,128)(2,1)}), bf16[512,2048]{0,1:T(8,128)(2,1)}) %all-gather.9.cloned.1.call-update) | async-done | bytes 2097168 | tf_op jit(solution)/shard_map/while/body/eval_jaxpr/all_gather | solution.py:52
  355.7 6.1 %fusion.30 = bf16[512,1024]{1,0:T(8,128)(2,1)} fusion(bf16[512,2048]{0,1:T(8,128)(2,1)} %all-gather.9.cloned.1.call-done, bf16[1,2048,1024]{2,1,0:T(8,128)(2,1)} %get-tuple-element.328), kind=kOutput, calls=%fused_computation.6.clone.1 | convolution fusion | flops 2148007936 | bytes 7340032 | tf_op jit(solution)/shard_map/while/body/eval_jaxpr/dot_general | solution.py:53
  361.9 0.0 all-gather.11.cloned.1.call-update
  361.9 81.7 %all-gather.11.cloned.1.call-done = bf16[2048,1024]{1,0:T(8,128)(2,1)} async-done(((bf16[512,1024]{1,0:T(8,128)(2,1)}), bf16[2048,1024]{1,0:T(8,128)(2,1)}) %all-gather.11.cloned.1.call-update) | async-done | bytes 4194320 | tf_op jit(solution)/shard_map/while/body/eval_jaxpr/all_gather | solution.py:67
  443.6 5.8 %fusion.31 = (bf16[512,1024]{0,1:T(8,128)(2,1)S(1)}, f32[512,1024]{0,1:T(8,128)S(1)}) fusion(bf16[2048,1024]{1,0:T(8,128)(2,1)} %all-gather.11.cloned.1.call-done, bf16[1,2048,512]{2,1,0:T(8,128)(2,1)} %get-tuple-element.329, f32[1,512,1024]{1,2,0:T(8,128)} %get-tuple-element.325), kind=kOutput, calls=%fused_computation.17.clone.1 | convolution fusion | flops 2148532224 | bytes 11534336 | tf_op jit(solution)/shard_map/while/body/eval_jaxpr/dot_general | solution.py:59
  449.4 0.7 bitcast_select_fusion.2
  450.2 1.8 copy.6
  (1 shorter events, 0.0 us)
Async XLA Ops:
  6.5 85.3 %all-gather.5.cloned.1.call-start = ((), (), s32[]{:S(2)}) async-start(), calls=%async_computation | async-start | bytes 5242880 | tf_op jit(solution)/shard_map/all_gather | solution.py:35
  7.3 165.5 %all-gather.7.cloned.1.call-start = ((), (), s32[]{:S(2)}) async-start(), calls=%async_computation.1 | async-start | bytes 5242880 | tf_op jit(solution)/shard_map/all_gather | solution.py:34
  94.9 83.4 %collective-permute-start.1 = (bf16[1,2048,512]{2,1,0:T(8,128)(2,1)}, bf16[1,2048,512]{2,1,0:T(8,128)(2,1)}, u32[]{:S(2)}, u32[]{:S(2)}) collective-permute-start(bf16[1,2048,512]{2,1,0:T(8,128)(2,1)} %constant_dynamic-slice_fusion.1), channel_id=1, source_target_pairs={{0,1},{1,0},{2,3},{3,2},{4,5},{5,4},{6,7},{7,6},{8,9},{9,8},{10,11... | collective-permute-start | bytes 6291464 | tf_op jit(solution)/shard_map/ppermute | solution.py:8
  175.8 9.5 %collective-permute-start.2 = (bf16[1,2048,512]{2,1,0:T(8,128)(2,1)}, bf16[1,2048,512]{2,1,0:T(8,128)(2,1)}, u32[]{:S(2)}, u32[]{:S(2)}) collective-permute-start(bf16[1,2048,512]{2,1,0:T(8,128)(2,1)} %constant_dynamic-slice_fusion), channel_id=1, source_target_pairs={{0,1},{1,0},{2,3},{3,2},{4,5},{5,4},{6,7},{7,6},{8,9},{9,8},{10,11... | collective-permute-start | bytes 6291464 | tf_op jit(solution)/shard_map/ppermute | solution.py:8
  178.2 7.0 %copy-start = (bf16[512,1024]{0,1:T(8,128)(2,1)}, bf16[512,1024]{0,1:T(8,128)(2,1)S(1)}, u32[]{:S(2)}) copy-start(bf16[512,1024]{0,1:T(8,128)(2,1)S(1)} %copy.4) | copy-start | bytes 3145732
  178.2 7.0 %copy-start.2 = (bf16[1,2048,1024]{2,1,0:T(8,128)(2,1)S(1)}, bf16[1,2048,1024]{2,1,0:T(8,128)(2,1)}, u32[]{:S(2)}) copy-start(bf16[1,2048,1024]{2,1,0:T(8,128)(2,1)} %all-gather.7.cloned.1.call-done) | copy-start | bytes 12582916
  185.3 3.9 copy-start.1
  189.2 35.2 %all-gather.9.cloned.1.call-start = ((), (), s32[]{:S(2)}) async-start(), calls=%async_computation.2 | async-start | bytes 3145728 | tf_op jit(solution)/shard_map/while/body/eval_jaxpr/all_gather | solution.py:52
  189.2 25.5 %collective-permute-start = (bf16[512,1024]{0,1:T(8,128)(2,1)S(1)}, bf16[512,1024]{0,1:T(8,128)(2,1)S(1)}, u32[]{:S(2)}, u32[]{:S(2)}) collective-permute-start(bf16[512,1024]{0,1:T(8,128)(2,1)S(1)} %get-tuple-element.312), channel_id=1, source_target_pairs={{8,0},{9,1},{10,2},{11,3},{12,4},{13,5},{14,6},{15,7},{24,16},{25,... | collective-permute-start | bytes 3145736 | tf_op jit(solution)/shard_map/while/body/eval_jaxpr/ppermute | solution.py:14
  215.8 96.4 %all-gather.11.cloned.1.call-start = ((), (), s32[]{:S(2)}) async-start(), calls=%async_computation.3 | async-start | bytes 5242880 | tf_op jit(solution)/shard_map/while/body/eval_jaxpr/all_gather | solution.py:67
  318.7 37.0 %all-gather.9.cloned.1.call-start = ((), (), s32[]{:S(2)}) async-start(), calls=%async_computation.2 | async-start | bytes 3145728 | tf_op jit(solution)/shard_map/while/body/eval_jaxpr/all_gather | solution.py:52
  318.8 25.9 %collective-permute-start = (bf16[512,1024]{0,1:T(8,128)(2,1)S(1)}, bf16[512,1024]{0,1:T(8,128)(2,1)S(1)}, u32[]{:S(2)}, u32[]{:S(2)}) collective-permute-start(bf16[512,1024]{0,1:T(8,128)(2,1)S(1)} %get-tuple-element.312), channel_id=1, source_target_pairs={{8,0},{9,1},{10,2},{11,3},{12,4},{13,5},{14,6},{15,7},{24,16},{25,... | collective-permute-start | bytes 3145736 | tf_op jit(solution)/shard_map/while/body/eval_jaxpr/ppermute | solution.py:14
  345.8 97.8 %all-gather.11.cloned.1.call-start = ((), (), s32[]{:S(2)}) async-start(), calls=%async_computation.3 | async-start | bytes 5242880 | tf_op jit(solution)/shard_map/while/body/eval_jaxpr/all_gather | solution.py:67
Sparse Core Ops, SparseCore 0:
  8.9 82.8 all-gather.4
  93.4 79.2 all-gather.6
  215.9 8.3 all-gather.8
  230.6 81.5 all-gather.10
  346.0 9.7 all-gather.8
  362.0 81.5 all-gather.10
where the time goes:
time: 460 us; the launch traced here: 459 us
  waiting for transfers between devices  393 us (85%)
  matrix products  30.9 us (7%)
  between operations  13.5 us (3%)
  local copies, waits for them, and re-layouts  9.71 us (2%)
  other arithmetic  7.51 us (2%)
    all_gather x2, waiting for transfers between devices, run_segment(): lax.all_gather(image, 'row', axis=0, tiled=True)  163 us
    all_gather x1, waiting for transfers between devices, local(): lax.all_gather(inverses, 'row', axis=1, tiled=True)  83.8 us
    all_gather x1, waiting for transfers between devices, local(): lax.all_gather(factors, 'row', axis=1, tiled=True)  77.2 us
    ppermute x2, waiting for transfers between devices, passed_along(): lax.ppermute(value, axis, [(source, source + steps) for source in range(f...  48.9 us
    all_gather x2, waiting for transfers between devices, run_segment(): state_full = lax.all_gather(current, 'col', axis=1, tiled=True)  18.3 us
    dot_general x2, matrix products, run_segment(): jnp.dot(state_full, factor_full[0], preferred_element_type=jnp.float32)  12.3 us
    dot_general x2, matrix products, accumulate(): lax.dot_general(left_panel, incoming_rows, (((0,), (0,)), ((), ())), pref...  11.6 us
  transfers between devices with their start and end apart: 10, of which 8 were waited for; matrix products, arithmetic and copies ran while one was open for 3% of the time, Pallas kernels for 0%

commit v1 on v0

v1 whole, which is shorter than its diff:
```python
import jax
import jax.numpy as jnp
from jax import lax
from jax.sharding import PartitionSpec as P


def partner(shard, axis, stride):
    return lax.ppermute(shard, axis, [(i, i ^ 1 << stride) for i in range(lax.axis_size(axis))])


def passed_along(value, axis, steps):
    count = lax.axis_size(axis)
    first, last = (max(0, -steps), min(count, count - steps))
    return lax.ppermute(value, axis, [(source, source + steps) for source in range(first, last)])


def local(factors, inverses, sigma_end):
    row_size = lax.axis_size("row")
    col_size = lax.axis_size("col")
    sec_size = lax.axis_size("sec")
    row_index = lax.axis_index("row")
    col_index = lax.axis_index("col")
    sec_index = lax.axis_index("sec")
    _, tile_rows, _ = factors.shape
    per_column = row_size // col_size
    offset = row_index % per_column * tile_rows
    owns_panel = col_index == row_index // per_column

    def gather(tile):
        return lax.all_gather(tile, "row", axis=0, tiled=True)

    def left_of(full):
        mine = lax.dynamic_slice_in_dim(full, offset, tile_rows, 1)
        return jnp.where(owns_panel, mine, partner(mine, "col", 0))

    def cross(left, full):
        return lax.dot_general(
            left, full, (((0,), (0,)), ((), ())), preferred_element_type=jnp.float32
        )

    current = sigma_end.astype(jnp.bfloat16)
    factor = gather(factors[0])
    state = gather(current)
    inverse = gather(inverses[0])
    factor_left = left_of(factor)
    diagonal = cross(left_of(inverse), inverse)
    result = None
    for segment in range(sec_size):
        half = cross(factor_left, state).astype(jnp.bfloat16)
        whole = lax.all_gather(half, "col", axis=1, tiled=True)
        block = diagonal + jnp.dot(whole, factor, preferred_element_type=jnp.float32)
        active = sec_index == sec_size - 1 - segment
        result = block if result is None else jnp.where(active, block, result)
        if segment < sec_size - 1:
            state = gather(passed_along(block.astype(jnp.bfloat16), "sec", -1))
    return result[None]


def solution(mesh):
    in_specs = (
        P(("groups", "sec"), "row", "col"),
        P(("groups", "sec"), "row", "col"),
        P(("groups", "row"), "col"),
    )
    out_specs = P(("groups", "sec"), "row", "col")
    return jax.shard_map(local, mesh=mesh, in_specs=in_specs, out_specs=out_specs, check_vma=False)
```

time: 460 us -> 416 us (0.904)
  waiting for transfers between devices: 393 us -> 357 us
  other arithmetic: 7.51 us -> 2.75 us
    ppermute x2 -> x1, waiting for transfers between devices: 48.9 us -> 25 us  [passed_along(): lax.ppermute(value, axis, [(source, source + steps) for source in range(f...]
    all_gather x6, waiting for transfers between devices: 343 us -> 331 us  [the longest x4 318 us: gather(): return lax.all_gather(tile, 'row', axis=0, tiled=True)]
    select_n x5 -> x0, other arithmetic: 7.51 us -> none  [the longest x1 3.88 us: local(): factor_left = jnp.where(owns_panel, local_pair[0], partner_pair[0])]
  transfers between devices with their start and end apart: 10 -> 9, of which waited for: 8 -> 7; matrix products, arithmetic and copies ran while one was open for 3% -> 5% of each run, Pallas kernels for 0% -> 0%
where the time goes in v1:
time: 416 us; the launch traced here: 415 us
  waiting for transfers between devices  357 us (86%)
  matrix products  33.2 us (8%)
  between operations  13.5 us (3%)
  local copies, waits for them, and re-layouts  5.75 us (1%)
    all_gather x4, waiting for transfers between devices, gather(): return lax.all_gather(tile, 'row', axis=0, tiled=True)  318 us
    ppermute x1, waiting for transfers between devices, passed_along(): lax.ppermute(value, axis, [(source, source + steps) for source in range(f...  25 us
    dot_general x3, matrix products, cross(): lax.dot_general(left, full, (((0,), (0,)), ((), ())), preferred_element_t...  18.9 us
    dot_general x2, matrix products, local(): jnp.dot(whole, factor, preferred_element_type=jnp.float32)  14.2 us
    all_gather x2, waiting for transfers between devices, local(): whole = lax.all_gather(half, 'col', axis=1, tiled=True)  12.6 us
  transfers between devices with their start and end apart: 9, of which 7 were waited for; matrix products, arithmetic and copies ran while one was open for 5% of the time, Pallas kernels for 0%

profile of v1, /device:TPU:1, one launch (start us, length us, event | category | flops | bytes accessed | tf_op | source)
XLA Modules:
  0.0 415.4 jit_solution(8728628893357089546)
XLA Ops:
  6.5 0.0 all-gather.19.cloned.1.call-start
  6.5 0.7 all-gather.19.cloned.1.call-update
  7.3 0.0 all-gather.17.cloned.1.call-start
  7.3 0.7 all-gather.17.cloned.1.call-update
  8.0 0.0 all-gather.9.cloned.1.call-start
  8.1 2.8 convert_element_type.12
  10.8 0.0 all-gather.9.cloned.1.call-update
  10.8 0.0 all-gather.11.cloned.1.call-start
  10.9 80.9 %all-gather.19.cloned.1.call-done = bf16[1,2048,1024]{2,1,0:T(8,128)(2,1)} async-done(((bf16[1,512,1024]{2,1,0:T(8,128)(2,1)}), bf16[1,2048,1024]{2,1,0:T(8,128)(2,1)}) %all-gather.19.cloned.1.call-update) | async-done | bytes 4194320 | tf_op jit(solution)/shard_map/all_gather | solution.py:30
  91.8 1.7 dynamic-slice_bitcast_fusion
  93.5 0.7 collective-permute-start.1
  94.3 78.4 %all-gather.17.cloned.1.call-done = bf16[1,2048,1024]{2,1,0:T(8,128)(2,1)} async-done(((bf16[1,512,1024]{2,1,0:T(8,128)(2,1)}), bf16[1,2048,1024]{2,1,0:T(8,128)(2,1)}) %all-gather.17.cloned.1.call-update) | async-done | bytes 4194320 | tf_op jit(solution)/shard_map/all_gather | solution.py:30
  172.7 3.0 dynamic-slice_bitcast_fusion.1
  175.8 0.7 collective-permute-start
  176.4 77.2 %all-gather.9.cloned.1.call-done = bf16[2048,1024]{1,0:T(8,128)(2,1)} async-done(((bf16[512,1024]{1,0:T(8,128)(2,1)}), bf16[2048,1024]{1,0:T(8,128)(2,1)}) %all-gather.9.cloned.1.call-update) | async-done | bytes 4194320 | tf_op jit(solution)/shard_map/all_gather | solution.py:30
  253.6 0.0 collective-permute-done.1
  253.6 6.2 %convolution_convert_fusion.1 = bf16[512,1024]{1,0:T(8,128)(2,1)} fusion(bf16[2048,1024]{1,0:T(8,128)(2,1)} %all-gather.9.cloned.1.call-done, bf16[2048,512]{1,0:T(8,128)(2,1)S(1)} %dynamic-slice_bitcast_fusion, bf16[2048,512]{1,0:T(8,128)(2,1)} %collective-permute-done.1, pred[]{:T(512)S(6)} %eq.9), kind=kOutput, calls=%fused_computation.14 | convolution fusion | flops 2149056512 | bytes 9437185 | tf_op jit(solution)/shard_map/dot_general | solution.py:37
  259.8 0.0 all-gather.11.cloned.1.call-update
  259.8 0.0 all-gather.13.cloned.1.call-start
  259.9 0.0 collective-permute-done
  259.9 6.6 %fusion.4 = f32[512,1024]{1,0:T(8,128)} fusion(bf16[1,2048,1024]{2,1,0:T(8,128)(2,1)} %all-gather.17.cloned.1.call-done, bf16[2048,512]{1,0:T(8,128)(2,1)} %dynamic-slice_bitcast_fusion.1, bf16[2048,512]{1,0:T(8,128)(2,1)} %collective-permute-done, pred[]{:T(512)S(6)} %eq.9), kind=kOutput, calls=%fused_computation.4 | convolution fusion | flops 2148532224 | bytes 10485761 | tf_op jit(solution)/shard_map/dot_general | solution.py:37
  266.5 3.0 all-gather.11.cloned.1.call-done
  269.5 7.1 %fusion.13 = (bf16[512,1024]{1,0:T(8,128)(2,1)S(1)}, f32[512,1024]{1,0:T(8,128)}) fusion(f32[512,1024]{1,0:T(8,128)} %fusion.4, bf16[512,2048]{1,0:T(8,128)(2,1)} %all-gather.11.cloned.1.call-done, bf16[1,2048,1024]{2,1,0:T(8,128)(2,1)} %all-gather.19.cloned.1.call-done), kind=kOutput, calls=%fused_computation.15 | convolution fusion | flops 2148532224 | bytes 11534336 | tf_op jit(solution)/shard_map/dot_general | solution.py:51
  276.6 1.3 collective-permute-start.2
  277.9 25.0 %collective-permute-done.2 = bf16[512,1024]{1,0:T(8,128)(2,1)S(1)} collective-permute-done((bf16[512,1024]{1,0:T(8,128)(2,1)S(1)}, bf16[512,1024]{1,0:T(8,128)(2,1)S(1)}, u32[]{:S(2)}, u32[]{:S(2)}) %collective-permute-start.2) | collective-permute-done | bytes 1048608 | tf_op jit(solution)/shard_map/ppermute | solution.py:14
  302.9 0.0 copy-start
  302.9 1.0 copy-done
  303.9 0.0 all-gather.13.cloned.1.call-update
  303.9 0.0 all-gather.15.cloned.1.call-start
  304.0 81.7 %all-gather.13.cloned.1.call-done = bf16[2048,1024]{1,0:T(8,128)(2,1)} async-done(((bf16[512,1024]{1,0:T(8,128)(2,1)}), bf16[2048,1024]{1,0:T(8,128)(2,1)}) %all-gather.13.cloned.1.call-update) | async-done | bytes 4194320 | tf_op jit(solution)/shard_map/all_gather | solution.py:30
  385.6 6.2 %convolution_convert_fusion = bf16[512,1024]{1,0:T(8,128)(2,1)} fusion(bf16[2048,1024]{1,0:T(8,128)(2,1)} %all-gather.13.cloned.1.call-done, bf16[2048,512]{1,0:T(8,128)(2,1)S(1)} %dynamic-slice_bitcast_fusion, bf16[2048,512]{1,0:T(8,128)(2,1)} %collective-permute-done.1, pred[]{:T(512)S(6)} %eq.9), kind=kOutput, calls=%fused_computation.13 | convolution fusion | flops 2149056512 | bytes 9437185 | tf_op jit(solution)/shard_map/dot_general | solution.py:37
  391.8 0.0 all-gather.15.cloned.1.call-update
  391.8 9.6 %all-gather.15.cloned.1.call-done = bf16[512,2048]{1,0:T(8,128)(2,1)} async-done(((bf16[512,1024]{1,0:T(8,128)(2,1)}), bf16[512,2048]{1,0:T(8,128)(2,1)}) %all-gather.15.cloned.1.call-update) | async-done | bytes 2097168 | tf_op jit(solution)/shard_map/all_gather | solution.py:50
  401.5 7.1 %select_bitcast_fusion = f32[1,512,1024]{2,1,0:T(8,128)} fusion(f32[512,1024]{1,0:T(8,128)} %get-tuple-element.6, f32[512,1024]{1,0:T(8,128)} %fusion.4, bf16[512,2048]{1,0:T(8,128)(2,1)} %all-gather.15.cloned.1.call-done, bf16[1,2048,1024]{2,1,0:T(8,128)(2,1)} %all-gather.19.cloned.1.call-done, pred[]{:T(512)S(6)} %eq.8), kind=kOutput, calls=%fused_computation.8 | convolution fusion | flops 2148532224 | bytes 12582913 | tf_op jit(solution)/shard_map/dot_general | solution.py:51
Async XLA Ops:
  6.5 85.3 %all-gather.19.cloned.1.call-start = ((), (), s32[]{:S(2)}) async-start(), calls=%async_computation.5 | async-start | bytes 5242880 | tf_op jit(solution)/shard_map/all_gather | solution.py:30
  7.3 165.5 %all-gather.17.cloned.1.call-start = ((), (), s32[]{:S(2)}) async-start(), calls=%async_computation.4 | async-start | bytes 5242880 | tf_op jit(solution)/shard_map/all_gather | solution.py:30
  8.0 245.6 %all-gather.9.cloned.1.call-start = ((), (), s32[]{:S(2)}) async-start(), calls=%async_computation | async-start | bytes 5242880 | tf_op jit(solution)/shard_map/all_gather | solution.py:30
  10.8 258.6 %all-gather.11.cloned.1.call-start = ((), (), s32[]{:S(2)}) async-start(), calls=%async_computation.1 | async-start | bytes 3145728 | tf_op jit(solution)/shard_map/all_gather | solution.py:50
  93.5 160.1 %collective-permute-start.1 = (bf16[2048,512]{1,0:T(8,128)(2,1)S(1)}, bf16[2048,512]{1,0:T(8,128)(2,1)}, u32[]{:S(2)}, u32[]{:S(2)}) collective-permute-start(bf16[2048,512]{1,0:T(8,128)(2,1)S(1)} %dynamic-slice_bitcast_fusion), channel_id=1, source_target_pairs={{0,1},{1,0},{2,3},{3,2},{4,5},{5,4},{6,7},{7,6},{8,9},{9,8},{10,11... | collective-permute-start | bytes 6291464 | tf_op jit(solution)/shard_map/ppermute | solution.py:8
  175.8 84.1 %collective-permute-start = (bf16[2048,512]{1,0:T(8,128)(2,1)}, bf16[2048,512]{1,0:T(8,128)(2,1)}, u32[]{:S(2)}, u32[]{:S(2)}) collective-permute-start(bf16[2048,512]{1,0:T(8,128)(2,1)} %dynamic-slice_bitcast_fusion.1), channel_id=1, source_target_pairs={{0,1},{1,0},{2,3},{3,2},{4,5},{5,4},{6,7},{7,6},{8,9},{9,8},{10,11... | collective-permute-start | bytes 6291464 | tf_op jit(solution)/shard_map/ppermute | solution.py:8
  259.8 125.8 %all-gather.13.cloned.1.call-start = ((), (), s32[]{:S(2)}) async-start(), calls=%async_computation.2 | async-start | bytes 5242880 | tf_op jit(solution)/shard_map/all_gather | solution.py:30
  276.6 26.3 %collective-permute-start.2 = (bf16[512,1024]{1,0:T(8,128)(2,1)S(1)}, bf16[512,1024]{1,0:T(8,128)(2,1)S(1)}, u32[]{:S(2)}, u32[]{:S(2)}) collective-permute-start(bf16[512,1024]{1,0:T(8,128)(2,1)S(1)} %get-tuple-element.5), channel_id=1, source_target_pairs={{8,0},{9,1},{10,2},{11,3},{12,4},{13,5},{14,6},{15,7},{24,16},{25,... | collective-permute-start | bytes 3145736 | tf_op jit(solution)/shard_map/ppermute | solution.py:14
  302.9 1.0 copy-start
  303.9 97.5 %all-gather.15.cloned.1.call-start = ((), (), s32[]{:S(2)}) async-start(), calls=%async_computation.3 | async-start | bytes 3145728 | tf_op jit(solution)/shard_map/all_gather | solution.py:50
Sparse Core Ops, SparseCore 0:
  8.9 82.8 all-gather.18
  93.4 79.2 all-gather.16
  174.3 79.2 all-gather.8
  259.9 9.4 all-gather.10
  304.0 81.5 all-gather.12
  392.0 9.4 all-gather.14

commit v2 on v1

--- a/solution.py
+++ b/solution.py
@@ -1,6 +1,8 @@
 import jax
 import jax.numpy as jnp
 from jax import lax
+from jax.experimental import pallas as pl
+from jax.experimental.pallas import tpu as pltpu
 from jax.sharding import PartitionSpec as P
 
 
@@ -56,11 +58,281 @@
     return result[None]
 
 
+FAC, INV, SIG, STA = range(4)
+DOWN, UP = range(2)
+MESH = pl.DeviceIdType.MESH
+TA = (((0,), (0,)), ((), ()))
+
+
+def kernel(n, f_ref, g_ref, s_ref, out, fb, gb, sb, xb, fl, gl, zb, ssem, rsem, hop_s, hop_x, left_s, left_r, z_s, z_r):
+    r = lax.axis_index("row")
+    c = lax.axis_index("col")
+    sec = lax.axis_index("sec")
+    t = f_ref.shape[1]
+    lower, upper = r > 0, r < n - 1
+    bufs = {FAC: fb, INV: gb, SIG: sb, STA: xb}
+    lefts = (fl, gl)
+    owner = c == r // 2
+    hl = r % 2
+
+    barrier = pltpu.get_barrier_semaphore()
+    pl.semaphore_signal(barrier, inc=1, device_id={"col": 1 - c}, device_id_type=MESH)
+    pl.semaphore_signal(barrier, inc=1, device_id={"sec": 1 - sec}, device_id_type=MESH)
+
+    @pl.when(lower)
+    def _():
+        pl.semaphore_signal(barrier, inc=1, device_id={"row": r - 1}, device_id_type=MESH)
+
+    @pl.when(upper)
+    def _():
+        pl.semaphore_signal(barrier, inc=1, device_id={"row": r + 1}, device_id_type=MESH)
+
+    pl.semaphore_wait(barrier, 2 + lower.astype(jnp.int32) + upper.astype(jnp.int32))
+
+    def rows(k):
+        return pl.ds(pl.multiple_of(k * t, t), t)
+
+    def cols(h):
+        return pl.ds(h * t, t)
+
+    def along(a, k, h, way):
+        piece = bufs[a].at[h, rows(k), :]
+        to = r - 1 if way == DOWN else r + 1
+        return pltpu.make_async_remote_copy(
+            src_ref=piece,
+            dst_ref=piece,
+            send_sem=ssem.at[a, h, k, way],
+            recv_sem=rsem.at[a, h, k],
+            device_id={"row": to},
+            device_id_type=MESH,
+        )
+
+    def hop_sigma(k):
+        piece = sb.at[0, rows(k), :]
+        return pltpu.make_async_remote_copy(
+            src_ref=piece, dst_ref=piece, send_sem=hop_s.at[k], recv_sem=rsem.at[SIG, 0, k],
+            device_id={"sec": 1}, device_id_type=MESH,
+        )
+
+    def hop_state(h):
+        piece = xb.at[h, rows(r), :]
+        return pltpu.make_async_remote_copy(
+            src_ref=piece, dst_ref=piece, send_sem=hop_x.at[h], recv_sem=rsem.at[STA, h, r],
+            device_id={"sec": 0}, device_id_type=MESH,
+        )
+
+    def to_left(a, k):
+        return pltpu.make_async_remote_copy(
+            src_ref=bufs[a].at[hl, rows(k), :], dst_ref=lefts[a].at[rows(k), :],
+            send_sem=left_s.at[a, k], recv_sem=left_r.at[a, k],
+            device_id={"col": 1 - c}, device_id_type=MESH,
+        )
+
+    def flows(a, k, h, way):
+        if a != INV:
+            return True
+        return (2 * c + h <= k) if way == DOWN else False
+
+    def when(*terms):
+        total = True
+        for term in terms:
+            if term is False:
+                return lambda f: None
+            if term is not True:
+                total = term if total is True else jnp.logical_and(total, term)
+        return pl.when(total)
+
+    def start_own(a, h):
+        @when(lower, flows(a, r, h, DOWN))
+        def _():
+            along(a, r, h, DOWN).start()
+
+        @when(upper, flows(a, r, h, UP))
+        def _():
+            along(a, r, h, UP).start()
+
+    def receive(a, h, d, then=None):
+        for way, k, edge in ((DOWN, r + d, lower), (UP, r - d, upper)):
+            @when(k < n if way == DOWN else k >= 0, flows(a, k, h, way))
+            def _():
+                along(a, k, h, way).wait_recv()
+
+                @pl.when(edge)
+                def _():
+                    along(a, k, h, way).start()
+
+                if then is not None:
+                    then(k)
+
+    def finish(a, h, ways=(DOWN, UP)):
+        for k in range(n):
+            for way in ways:
+                side = jnp.logical_and(lower, r <= k) if way == DOWN else jnp.logical_and(upper, r >= k)
+
+                @when(side, flows(a, k, h, way))
+                def _():
+                    along(a, k, h, way).wait_send()
+
+    def share_left(a, k):
+        @pl.when(owner)
+        def _():
+            to_left(a, k).start()
+            lefts[a][rows(k), :] = bufs[a][hl, rows(k), :]
+
+    for h in range(2):
+        sb[h, rows(r), :] = s_ref[:, cols(h)].astype(jnp.bfloat16)
+    start_own(SIG, sec)
+    for h in range(2):
+        fb[h, rows(r), :] = f_ref[0, :, cols(h)]
+        start_own(FAC, h)
+    for h in range(2):
+        gb[h, rows(r), :] = g_ref[0, :, cols(h)]
+        start_own(INV, h)
+    share_left(FAC, r)
+    share_left(INV, r)
+
+    for k in range(n):
+        @pl.when(k < r)
+        def _():
+            gl[rows(k), :] = jnp.zeros((t, t), jnp.bfloat16)
+        for h in range(2):
+            @pl.when(jnp.logical_or(k < r, jnp.logical_and(k != r, k < 2 * c + h)))
+            def _():
+                gb[h, rows(k), :] = jnp.zeros((t, t), jnp.bfloat16)
+
+    def pass_sigma(k):
+        @pl.when(sec == 0)
+        def _():
+            hop_sigma(k).start()
+
+    for d in range(1, n):
+        receive(SIG, sec, d, pass_sigma)
+        for h in range(2):
+            receive(FAC, h, d)
+        for k, inside in ((r + d, r + d < n), (r - d, r - d >= 0)):
+            @pl.when(inside)
+            def _():
+                share_left(FAC, k)
+        for h in range(2):
+            receive(INV, h, d)
+
+        @pl.when(r + d < n)
+        def _():
+            share_left(INV, r + d)
+
+    @pl.when(jnp.logical_not(owner))
+    def _():
+        for k in range(n):
+            to_left(FAC, k).wait_recv()
+
+            @pl.when(k >= r)
+            def _():
+                to_left(INV, k).wait_recv()
+
+    for h in range(2):
+        out[0, :, cols(h)] = lax.dot_general(gl[...], gb[h], TA, preferred_element_type=jnp.float32)
+
+    def send_z():
+        piece = zb.at[c]
+        return pltpu.make_async_remote_copy(
+            src_ref=piece, dst_ref=piece, send_sem=z_s, recv_sem=z_r,
+            device_id={"col": 1 - c}, device_id_type=MESH,
+        )
+
+    def products(buf, then):
+        for h in range(2):
+            zb[c, :, cols(h)] = lax.dot_general(
+                fl[...], buf[h], TA, preferred_element_type=jnp.float32
+            ).astype(jnp.bfloat16)
+        send_z().start()
+        send_z().wait_recv()
+        for h in range(2):
+            total = out[0, :, cols(h)]
+            for j in range(2):
+                total += jnp.dot(zb[j], fb[h, j * 2 * t:(j + 1) * 2 * t, :], preferred_element_type=jnp.float32)
+            out[0, :, cols(h)] = total
+            then(h, total)
+
+    @pl.when(sec == 1)
+    def _():
+        for k in range(n):
+            @pl.when(k != r)
+            def _():
+                hop_sigma(k).wait_recv()
+
+        def onward(h, total):
+            xb[h, rows(r), :] = total.astype(jnp.bfloat16)
+            hop_state(h).start()
+
+        products(sb, onward)
+        for h in range(2):
+            hop_state(h).wait_send()
+
+    @pl.when(sec == 0)
+    def _():
+        for h in range(2):
+            hop_state(h).wait_recv()
+            start_own(STA, h)
+        for d in range(1, n):
+            for h in range(2):
+                receive(STA, h, d)
+        products(xb, lambda h, total: None)
+        for h in range(2):
+            finish(STA, h)
+        for k in range(n):
+            @pl.when(k != r)
+            def _():
+                hop_sigma(k).wait_send()
+
+    send_z().wait_send()
+    finish(SIG, sec)
+    for h in range(2):
+        finish(FAC, h)
+        finish(INV, h, (DOWN,))
+
+    @pl.when(owner)
+    def _():
+        for k in range(n):
+            to_left(FAC, k).wait_send()
+
+            @pl.when(k >= r)
+            def _():
+                to_left(INV, k).wait_send()
+
+
+def fused(factors, inverses, sigma_end):
+    n = lax.axis_size("row")
+    _, t, width = factors.shape
+    low = jnp.bfloat16
+    dma = pltpu.SemaphoreType.DMA
+    vmem = pl.BlockSpec(memory_space=pltpu.VMEM)
+    wide = pltpu.VMEM((2, n * t, t), low)
+    return pl.pallas_call(
+        lambda *refs: kernel(n, *refs),
+        out_shape=jax.ShapeDtypeStruct((1, t, width), jnp.float32),
+        in_specs=[vmem] * 3,
+        out_specs=vmem,
+        scratch_shapes=[
+            wide, wide, wide, wide,
+            pltpu.VMEM((n * t, t), low),
+            pltpu.VMEM((n * t, t), low),
+            pltpu.VMEM((2, t, 2 * t), low),
+            dma((4, 2, n, 2)), dma((4, 2, n)), dma((n,)), dma((2,)),
+            dma((2, n)), dma((2, n)), dma(()), dma(()),
+        ],
+        compiler_params=pltpu.CompilerParams(
+            collective_id=0, has_side_effects=True, vmem_limit_bytes=56 * 2**20
+        ),
+    )(factors, inverses, sigma_end)
+
+
 def solution(mesh):
     in_specs = (
         P(("groups", "sec"), "row", "col"),
         P(("groups", "sec"), "row", "col"),
         P(("groups", "row"), "col"),
     )
+    fits = mesh.shape["sec"] == 2 and mesh.shape["row"] == 2 * mesh.shape["col"] == 4
+    body = fused if fits else local
     out_specs = P(("groups", "sec"), "row", "col")
-    return jax.shard_map(local, mesh=mesh, in_specs=in_specs, out_specs=out_specs, check_vma=False)
+    return jax.shard_map(body, mesh=mesh, in_specs=in_specs, out_specs=out_specs, check_vma=False)

time: 416 us -> 240 us (0.58)
  waiting for transfers between devices: 357 us -> 0 us
  Pallas kernels: 0 us -> 236 us
  matrix products: 33.2 us -> 0 us
  between operations: 13.5 us -> 0.01 us
    all_gather x6 -> x0, waiting for transfers between devices: 331 us -> none  [the longest x4 318 us: gather(): return lax.all_gather(tile, 'row', axis=0, tiled=True)]
    pallas_call x0 -> x1, Pallas kernels: none -> 236 us  [fused(): pl.pallas_call(lambda *refs: kernel(n, *refs), out_shape=jax.ShapeDtypeSt...]
    dot_general x5 -> x0, matrix products: 33.2 us -> none  [the longest x3 18.9 us: cross(): lax.dot_general(left, full, (((0,), (0,)), ((), ())), preferred_element_t...]
    ppermute x3 -> x0, waiting for transfers between devices: 25.1 us -> none  [the longest x1 25 us: passed_along(): lax.ppermute(value, axis, [(source, source + steps) for source in range(f...]
    dynamic_slice x2 -> x0, local copies, waits for them, and re-layouts: 4.77 us -> none  [left_of(): mine = lax.dynamic_slice_in_dim(full, offset, tile_rows, 1)]
  transfers between devices with their start and end apart: 9 -> 0, of which waited for: 7 -> 0; matrix products, arithmetic and copies ran while one was open for 5% -> 0% of each run, Pallas kernels for 0% -> 0%
where the time goes in v2:
time: 240 us
  Pallas kernels  236 us (98%)
  local copies, waits for them, and re-layouts  3.16 us (1%)
    pallas_call x1, Pallas kernels, fused(): pl.pallas_call(lambda *refs: kernel(n, *refs), out_shape=jax.ShapeDtypeSt...  236 us

profile of v2, /device:TPU:1, one launch (start us, length us, event | category | flops | bytes accessed | tf_op | source)
XLA Modules:
  0.0 239.6 jit_solution(7481970437366688981)
XLA Ops:
  0.0 236.5 %shard_map.37 = f32[1,512,1024]{2,1,0:T(8,128)} custom-call(bf16[1,512,1024]{2,1,0:T(8,128)(2,1)} %refs_0_.1, bf16[1,512,1024]{2,1,0:T(8,128)(2,1)} %refs_1_.1, f32[512,1024]{1,0:T(8,128)} %refs_2_.1), custom_call_target="tpu_custom_call" | custom-call | tf_op jit(solution)/shard_map/pallas_call | solution.py:310
  236.5 3.2 %copy.5 = f32[1,512,1024]{2,1,0:T(8,128)} copy(f32[1,512,1024]{2,1,0:T(8,128)} %shard_map.37) | data formatting | bytes 4194304

commit v3 on v2

--- a/solution.py
+++ b/solution.py
@@ -64,16 +64,19 @@
 TA = (((0,), (0,)), ((), ()))
 
 
-def kernel(n, f_ref, g_ref, s_ref, out, fb, gb, sb, xb, fl, gl, zb, ssem, rsem, hop_s, hop_x, left_s, left_r, z_s, z_r):
+def kernel(n, f_ref, g_ref, s_ref, out, fb, gb, sb, xb, fl, gl, g0, db, zb, ssem, rsem, hop_s, hop_x, left_s, left_r, end_s, end_r, z_s, z_r):
     r = lax.axis_index("row")
     c = lax.axis_index("col")
     sec = lax.axis_index("sec")
     t = f_ref.shape[1]
     lower, upper = r > 0, r < n - 1
+    below = {INV: r > 1}
     bufs = {FAC: fb, INV: gb, SIG: sb, STA: xb}
-    lefts = (fl, gl)
-    owner = c == r // 2
-    hl = r % 2
+    lefts = (fl, gl, g0)
+    sources = (fb, gb, gb)
+    owners = (c == r // 2, c == r // 2, jnp.logical_and(c == 0, r == 1))
+    picks = (r % 2, r % 2, 0)
+    spans = ((0, t), (0, t // 2), (t // 2, t // 2))
 
     barrier = pltpu.get_barrier_semaphore()
     pl.semaphore_signal(barrier, inc=1, device_id={"col": 1 - c}, device_id_type=MESH)
@@ -95,8 +98,12 @@
     def cols(h):
         return pl.ds(h * t, t)
 
+    def state_piece(p, k):
+        first, width = spans[p]
+        return xb.at[min(p, 1), rows(k), pl.ds(first, width)]
+
     def along(a, k, h, way):
-        piece = bufs[a].at[h, rows(k), :]
+        piece = state_piece(h, k) if a == STA else bufs[a].at[h, rows(k), :]
         to = r - 1 if way == DOWN else r + 1
         return pltpu.make_async_remote_copy(
             src_ref=piece,
@@ -114,16 +121,16 @@
             device_id={"sec": 1}, device_id_type=MESH,
         )
 
-    def hop_state(h):
-        piece = xb.at[h, rows(r), :]
-        return pltpu.make_async_remote_copy(
-            src_ref=piece, dst_ref=piece, send_sem=hop_x.at[h], recv_sem=rsem.at[STA, h, r],
+    def hop_state(p, k):
+        piece = state_piece(p, k)
+        return pltpu.make_async_remote_copy(
+            src_ref=piece, dst_ref=piece, send_sem=hop_x.at[p, k], recv_sem=rsem.at[STA, p, k],
             device_id={"sec": 0}, device_id_type=MESH,
         )
 
     def to_left(a, k):
         return pltpu.make_async_remote_copy(
-            src_ref=bufs[a].at[hl, rows(k), :], dst_ref=lefts[a].at[rows(k), :],
+            src_ref=sources[a].at[picks[a], rows(k), :], dst_ref=lefts[a].at[rows(k), :],
             send_sem=left_s.at[a, k], recv_sem=left_r.at[a, k],
             device_id={"col": 1 - c}, device_id_type=MESH,
         )
@@ -136,14 +143,14 @@
     def when(*terms):
         total = True
         for term in terms:
-            if term is False:
+            if term is False or (isinstance(term, bool) and not term):
                 return lambda f: None
             if term is not True:
                 total = term if total is True else jnp.logical_and(total, term)
         return pl.when(total)
 
     def start_own(a, h):
-        @when(lower, flows(a, r, h, DOWN))
+        @when(below.get(a, lower), flows(a, r, h, DOWN))
         def _():
             along(a, r, h, DOWN).start()
 
@@ -152,8 +159,8 @@
             along(a, r, h, UP).start()
 
     def receive(a, h, d, then=None):
-        for way, k, edge in ((DOWN, r + d, lower), (UP, r - d, upper)):
-            @when(k < n if way == DOWN else k >= 0, flows(a, k, h, way))
+        for way, k, edge in ((DOWN, r + d, below.get(a, lower)), (UP, r - d, upper)):
+            @when(k < n if way == DOWN else k >= 0, a != INV or lower, flows(a, k, h, way))
             def _():
                 along(a, k, h, way).wait_recv()
 
@@ -167,36 +174,33 @@
     def finish(a, h, ways=(DOWN, UP)):
         for k in range(n):
             for way in ways:
-                side = jnp.logical_and(lower, r <= k) if way == DOWN else jnp.logical_and(upper, r >= k)
+                side = jnp.logical_and(below.get(a, lower), r <= k) if way == DOWN else jnp.logical_and(upper, r >= k)
 
                 @when(side, flows(a, k, h, way))
                 def _():
                     along(a, k, h, way).wait_send()
 
     def share_left(a, k):
-        @pl.when(owner)
+        @pl.when(owners[a])
         def _():
             to_left(a, k).start()
-            lefts[a][rows(k), :] = bufs[a][hl, rows(k), :]
-
+            lefts[a][rows(k), :] = sources[a][picks[a], rows(k), :]
+
+    for h in range(2):
+        gb[h, rows(r), :] = g_ref[0, :, cols(h)]
+        start_own(INV, h)
     for h in range(2):
         sb[h, rows(r), :] = s_ref[:, cols(h)].astype(jnp.bfloat16)
     start_own(SIG, sec)
     for h in range(2):
         fb[h, rows(r), :] = f_ref[0, :, cols(h)]
         start_own(FAC, h)
-    for h in range(2):
-        gb[h, rows(r), :] = g_ref[0, :, cols(h)]
-        start_own(INV, h)
-    share_left(FAC, r)
-    share_left(INV, r)
-
-    for k in range(n):
-        @pl.when(k < r)
-        def _():
-            gl[rows(k), :] = jnp.zeros((t, t), jnp.bfloat16)
-        for h in range(2):
-            @pl.when(jnp.logical_or(k < r, jnp.logical_and(k != r, k < 2 * c + h)))
+    for a in range(3):
+        share_left(a, r)
+
+    for k in range(1, n):
+        for h in range(2):
+            @pl.when(jnp.logical_and(k > r, k < 2 * c + h))
             def _():
                 gb[h, rows(k), :] = jnp.zeros((t, t), jnp.bfloat16)
 
@@ -205,7 +209,47 @@
         def _():
             hop_sigma(k).start()
 
+    def cross(left, right):
+        return lax.dot_general(left, right, TA, preferred_element_type=jnp.float32)
+
+    def end_copy(h):
+        return pltpu.make_async_remote_copy(
+            src_ref=db.at[0, h], dst_ref=db.at[1, h], send_sem=end_s.at[h], recv_sem=end_r.at[h],
+            device_id={"row": 0}, device_id_type=MESH,
+        )
+
+    def diagonals():
+        for a, least in ((2, 1), (1, None)):
+            for k in range(1, n):
+                here = r == 1 if a == 2 else jnp.logical_and(lower, r <= k)
+
+                @when(jnp.logical_and(here, c != (0 if a == 2 else r // 2)))
+                def _():
+                    to_left(a, k).wait_recv()
+
+        @pl.when(r == 1)
+        def _():
+            for h in range(2):
+                db[0, h] = cross(g0[t:, :], gb[h, t:, :]).astype(jnp.bfloat16)
+                end_copy(h).start()
+
+        for first in range(1, n):
+            @pl.when(r == first)
+            def _():
+                for h in range(2):
+                    out[0, :, cols(h)] = cross(gl[first * t:, :], gb[h, first * t:, :])
+
     for d in range(1, n):
+        for h in range(2):
+            receive(INV, h, d)
+
+        @when(lower, r + d < n)
+        def _():
+            share_left(1, r + d)
+            share_left(2, r + d)
+
+        if d == n - 2:
+            diagonals()
         receive(SIG, sec, d, pass_sigma)
         for h in range(2):
             receive(FAC, h, d)
@@ -213,24 +257,21 @@
             @pl.when(inside)
             def _():
                 share_left(FAC, k)
-        for h in range(2):
-            receive(INV, h, d)
-
-        @pl.when(r + d < n)
-        def _():
-            share_left(INV, r + d)
-
-    @pl.when(jnp.logical_not(owner))
-    def _():
-        for k in range(n):
-            to_left(FAC, k).wait_recv()
-
-            @pl.when(k >= r)
-            def _():
-                to_left(INV, k).wait_recv()
-
-    for h in range(2):
-        out[0, :, cols(h)] = lax.dot_general(gl[...], gb[h], TA, preferred_element_type=jnp.float32)
+
+    @pl.when(jnp.logical_not(owners[0]))
+    def _():
+        for k in range(n):
+            to_left(0, k).wait_recv()
+
+    @pl.when(r == 0)
+    def _():
+        @pl.when(c == 1)
+        def _():
+            to_left(1, 0).wait_recv()
+
+        for h in range(2):
+            end_copy(h).wait_recv()
+            out[0, :, cols(h)] = cross(gl[:t, :], gb[h, :t, :]) + db[1, h].astype(jnp.float32)
 
     def send_z():
         piece = zb.at[c]
@@ -241,12 +282,10 @@
 
     def products(buf, then):
         for h in range(2):
-            zb[c, :, cols(h)] = lax.dot_general(
-                fl[...], buf[h], TA, preferred_element_type=jnp.float32
-            ).astype(jnp.bfloat16)
+            zb[c, :, cols(h)] = cross(fl[...], buf[h]).astype(jnp.bfloat16)
         send_z().start()
         send_z().wait_recv()
-        for h in range(2):
+        for h in (1, 0):
             total = out[0, :, cols(h)]
             for j in range(2):
                 total += jnp.dot(zb[j], fb[h, j * 2 * t:(j + 1) * 2 * t, :], preferred_element_type=jnp.float32)
@@ -262,23 +301,35 @@
 
         def onward(h, total):
             xb[h, rows(r), :] = total.astype(jnp.bfloat16)
-            hop_state(h).start()
+            if h == 1:
+                hop_state(1, r).start()
+                start_own(STA, 2)
+                hop_state(2, r).start()
+            else:
+                hop_state(0, r).start()
 
         products(sb, onward)
-        for h in range(2):
-            hop_state(h).wait_send()
+        for d in range(1, n):
+            receive(STA, 2, d, lambda k: hop_state(2, k).start())
+        finish(STA, 2)
+        hop_state(0, r).wait_send()
+        hop_state(1, r).wait_send()
+        for k in range(n):
+            hop_state(2, k).wait_send()
 
     @pl.when(sec == 0)
     def _():
-        for h in range(2):
-            hop_state(h).wait_recv()
-            start_own(STA, h)
+        for p in (1, 0):
+            hop_state(p, r).wait_recv()
+            start_own(STA, p)
         for d in range(1, n):
-            for h in range(2):
-                receive(STA, h, d)
+            for p in (1, 0):
+                receive(STA, p, d)
+        for k in range(n):
+            hop_state(2, k).wait_recv()
         products(xb, lambda h, total: None)
-        for h in range(2):
-            finish(STA, h)
+        for p in range(2):
+            finish(STA, p)
         for k in range(n):
             @pl.when(k != r)
             def _():
@@ -290,14 +341,23 @@
         finish(FAC, h)
         finish(INV, h, (DOWN,))
 
-    @pl.when(owner)
-    def _():
-        for k in range(n):
-            to_left(FAC, k).wait_send()
-
-            @pl.when(k >= r)
-            def _():
-                to_left(INV, k).wait_send()
+    @pl.when(r == 1)
+    def _():
+        for h in range(2):
+            end_copy(h).wait_send()
+
+    for k in range(n):
+        @pl.when(owners[0])
+        def _():
+            to_left(0, k).wait_send()
+
+        @when(jnp.logical_and(owners[1], jnp.logical_and(r <= k, jnp.logical_or(lower, k == 0))))
+        def _():
+            to_left(1, k).wait_send()
+
+        @when(owners[2], k >= 1)
+        def _():
+            to_left(2, k).wait_send()
 
 
 def fused(factors, inverses, sigma_end):
@@ -316,9 +376,11 @@
             wide, wide, wide, wide,
             pltpu.VMEM((n * t, t), low),
             pltpu.VMEM((n * t, t), low),
+            pltpu.VMEM((n * t, t), low),
+            pltpu.VMEM((2, 2, t, t), low),
             pltpu.VMEM((2, t, 2 * t), low),
-            dma((4, 2, n, 2)), dma((4, 2, n)), dma((n,)), dma((2,)),
-            dma((2, n)), dma((2, n)), dma(()), dma(()),
+            dma((4, 3, n, 2)), dma((4, 3, n)), dma((n,)), dma((3, n)),
+            dma((3, n)), dma((3, n)), dma((2,)), dma((2,)), dma(()), dma(()),
         ],
         compiler_params=pltpu.CompilerParams(
             collective_id=0, has_side_effects=True, vmem_limit_bytes=56 * 2**20

time: 240 us -> 217 us (0.904)
  Pallas kernels: 236 us -> 212 us
    pallas_call x1, Pallas kernels: 236 us -> 212 us  [fused(): pl.pallas_call(lambda *refs: kernel(n, *refs), out_shape=jax.ShapeDtypeSt...]
where the time goes in v3:
time: 217 us; the launch traced here: 215 us
  Pallas kernels  212 us (98%)
  local copies, waits for them, and re-layouts  3.16 us (1%)
    pallas_call x1, Pallas kernels, fused(): pl.pallas_call(lambda *refs: kernel(n, *refs), out_shape=jax.ShapeDtypeSt...  212 us

profile of v3, /device:TPU:1, one launch (start us, length us, event | category | flops | bytes accessed | tf_op | source)
XLA Modules:
  0.0 215.3 jit_solution(7096179010701954985)
XLA Ops:
  0.0 212.1 %shard_map.37 = f32[1,512,1024]{2,1,0:T(8,128)} custom-call(bf16[1,512,1024]{2,1,0:T(8,128)(2,1)} %refs_0_.1, bf16[1,512,1024]{2,1,0:T(8,128)(2,1)} %refs_1_.1, f32[512,1024]{1,0:T(8,128)} %refs_2_.1), custom_call_target="tpu_custom_call" | custom-call | tf_op jit(solution)/shard_map/pallas_call | solution.py:370
  212.2 3.2 %copy.5 = f32[1,512,1024]{2,1,0:T(8,128)} copy(f32[1,512,1024]{2,1,0:T(8,128)} %shard_map.37) | data formatting | bytes 4194304

commit v4 on v3

--- a/solution.py
+++ b/solution.py
@@ -64,7 +64,7 @@
 TA = (((0,), (0,)), ((), ()))
 
 
-def kernel(n, f_ref, g_ref, s_ref, out, fb, gb, sb, xb, fl, gl, g0, db, zb, ssem, rsem, hop_s, hop_x, left_s, left_r, end_s, end_r, z_s, z_r):
+def kernel(n, f_ref, g_ref, s_ref, out, fb, gb, sb, xb, fl, gl, g0, db, zb, zacc, ssem, rsem, hop_s, hop_x, left_s, left_r, end_s, end_r, z_s, z_r):
     r = lax.axis_index("row")
     c = lax.axis_index("col")
     sec = lax.axis_index("sec")
@@ -76,7 +76,10 @@
     sources = (fb, gb, gb)
     owners = (c == r // 2, c == r // 2, jnp.logical_and(c == 0, r == 1))
     picks = (r % 2, r % 2, 0)
-    spans = ((0, t), (0, t // 2), (t // 2, t // 2))
+    spans = {
+        SIG: ((0, t), (0, t // 2), (t // 2, t // 2)),
+        STA: ((0, t), (0, t // 4), (t // 4, t - t // 4)),
+    }
 
     barrier = pltpu.get_barrier_semaphore()
     pl.semaphore_signal(barrier, inc=1, device_id={"col": 1 - c}, device_id_type=MESH)
@@ -98,12 +101,14 @@
     def cols(h):
         return pl.ds(h * t, t)
 
-    def state_piece(p, k):
-        first, width = spans[p]
-        return xb.at[min(p, 1), rows(k), pl.ds(first, width)]
+    def piece_of(a, p, k):
+        if a not in spans:
+            return bufs[a].at[p, rows(k), :]
+        first, width = spans[a][p]
+        return bufs[a].at[min(p, 1), rows(k), pl.ds(first, width)]
 
     def along(a, k, h, way):
-        piece = state_piece(h, k) if a == STA else bufs[a].at[h, rows(k), :]
+        piece = piece_of(a, h, k)
         to = r - 1 if way == DOWN else r + 1
         return pltpu.make_async_remote_copy(
             src_ref=piece,
@@ -114,15 +119,15 @@
             device_id_type=MESH,
         )
 
-    def hop_sigma(k):
-        piece = sb.at[0, rows(k), :]
-        return pltpu.make_async_remote_copy(
-            src_ref=piece, dst_ref=piece, send_sem=hop_s.at[k], recv_sem=rsem.at[SIG, 0, k],
+    def hop_sigma(p, k):
+        piece = piece_of(SIG, p, k)
+        return pltpu.make_async_remote_copy(
+            src_ref=piece, dst_ref=piece, send_sem=hop_s.at[p, k], recv_sem=rsem.at[SIG, p, k],
             device_id={"sec": 1}, device_id_type=MESH,
         )
 
     def hop_state(p, k):
-        piece = state_piece(p, k)
+        piece = piece_of(STA, p, k)
         return pltpu.make_async_remote_copy(
             src_ref=piece, dst_ref=piece, send_sem=hop_x.at[p, k], recv_sem=rsem.at[STA, p, k],
             device_id={"sec": 0}, device_id_type=MESH,
@@ -187,11 +192,20 @@
             lefts[a][rows(k), :] = sources[a][picks[a], rows(k), :]
 
     for h in range(2):
+        sb[h, rows(r), :] = s_ref[:, cols(h)].astype(jnp.bfloat16)
+
+    @pl.when(sec == 0)
+    def _():
+        start_own(SIG, 0)
+        start_own(SIG, 1)
+
+    @pl.when(sec == 1)
+    def _():
+        start_own(SIG, 2)
+
+    for h in range(2):
         gb[h, rows(r), :] = g_ref[0, :, cols(h)]
         start_own(INV, h)
-    for h in range(2):
-        sb[h, rows(r), :] = s_ref[:, cols(h)].astype(jnp.bfloat16)
-    start_own(SIG, sec)
     for h in range(2):
         fb[h, rows(r), :] = f_ref[0, :, cols(h)]
         start_own(FAC, h)
@@ -204,10 +218,38 @@
             def _():
                 gb[h, rows(k), :] = jnp.zeros((t, t), jnp.bfloat16)
 
-    def pass_sigma(k):
+    def gather_sigma(d):
         @pl.when(sec == 0)
         def _():
-            hop_sigma(k).start()
+            for p in range(2):
+                receive(SIG, p, d, lambda k: hop_sigma(p, k).start())
+
+        @pl.when(sec == 1)
+        def _():
+            receive(SIG, 2, d)
+
+    def add_rows(buf, k, first=False):
+        for h in range(2):
+            part = cross(fl[rows(k), :], buf[h, rows(k), :])
+            zacc[h] = part if first else zacc[h] + part
+
+    def await_left(k):
+        @pl.when(jnp.logical_not(owners[0]))
+        def _():
+            to_left(0, k).wait_recv()
+
+    def ranked(d, then):
+        for k, inside in ((r + d, r + d < n), (r - d, r - d >= 0)):
+            @pl.when(inside)
+            def _():
+                then(k)
+
+    def add_sigma(k, first=False):
+        await_left(k)
+        if not first:
+            for p in range(2):
+                hop_sigma(p, k).wait_recv()
+        add_rows(sb, k, first)
 
     def cross(left, right):
         return lax.dot_general(left, right, TA, preferred_element_type=jnp.float32)
@@ -250,18 +292,24 @@
 
         if d == n - 2:
             diagonals()
-        receive(SIG, sec, d, pass_sigma)
+        gather_sigma(d)
         for h in range(2):
             receive(FAC, h, d)
-        for k, inside in ((r + d, r + d < n), (r - d, r - d >= 0)):
-            @pl.when(inside)
-            def _():
-                share_left(FAC, k)
-
-    @pl.when(jnp.logical_not(owners[0]))
+        ranked(d, lambda k: share_left(FAC, k))
+
+        @pl.when(sec == 1)
+        def _():
+            if d == n - 2:
+                add_sigma(r, True)
+                for e in range(1, d + 1):
+                    ranked(e, add_sigma)
+            elif d > n - 2:
+                ranked(d, add_sigma)
+
+    @pl.when(sec == 0)
     def _():
         for k in range(n):
-            to_left(0, k).wait_recv()
+            await_left(k)
 
     @pl.when(r == 0)
     def _():
@@ -273,18 +321,19 @@
             end_copy(h).wait_recv()
             out[0, :, cols(h)] = cross(gl[:t, :], gb[h, :t, :]) + db[1, h].astype(jnp.float32)
 
-    def send_z():
-        piece = zb.at[c]
-        return pltpu.make_async_remote_copy(
-            src_ref=piece, dst_ref=piece, send_sem=z_s, recv_sem=z_r,
+    def send_z(h):
+        piece = zb.at[c, :, cols(h)]
+        return pltpu.make_async_remote_copy(
+            src_ref=piece, dst_ref=piece, send_sem=z_s.at[h], recv_sem=z_r.at[h],
             device_id={"col": 1 - c}, device_id_type=MESH,
         )
 
-    def products(buf, then):
-        for h in range(2):
-            zb[c, :, cols(h)] = cross(fl[...], buf[h]).astype(jnp.bfloat16)
-        send_z().start()
-        send_z().wait_recv()
+    def products(then):
+        for h in range(2):
+            zb[c, :, cols(h)] = zacc[h].astype(jnp.bfloat16)
+            send_z(h).start()
+        for h in range(2):
+            send_z(h).wait_recv()
         for h in (1, 0):
             total = out[0, :, cols(h)]
             for j in range(2):
@@ -294,11 +343,6 @@
 
     @pl.when(sec == 1)
     def _():
-        for k in range(n):
-            @pl.when(k != r)
-            def _():
-                hop_sigma(k).wait_recv()
-
         def onward(h, total):
             xb[h, rows(r), :] = total.astype(jnp.bfloat16)
             if h == 1:
@@ -308,7 +352,7 @@
             else:
                 hop_state(0, r).start()
 
-        products(sb, onward)
+        products(onward)
         for d in range(1, n):
             receive(STA, 2, d, lambda k: hop_state(2, k).start())
         finish(STA, 2)
@@ -317,6 +361,10 @@
         for k in range(n):
             hop_state(2, k).wait_send()
 
+    def add_state(k, first=False):
+        hop_state(2, k).wait_recv()
+        add_rows(xb, k, first)
+
     @pl.when(sec == 0)
     def _():
         for p in (1, 0):
@@ -325,18 +373,29 @@
         for d in range(1, n):
             for p in (1, 0):
                 receive(STA, p, d)
-        for k in range(n):
-            hop_state(2, k).wait_recv()
-        products(xb, lambda h, total: None)
+            if d == n - 2:
+                add_state(r, True)
+                for e in range(1, d + 1):
+                    ranked(e, add_state)
+            elif d > n - 2:
+                ranked(d, add_state)
+        products(lambda h, total: None)
         for p in range(2):
             finish(STA, p)
         for k in range(n):
             @pl.when(k != r)
             def _():
-                hop_sigma(k).wait_send()
-
-    send_z().wait_send()
-    finish(SIG, sec)
+                for p in range(2):
+                    hop_sigma(p, k).wait_send()
+        for p in range(2):
+            finish(SIG, p)
+
+    @pl.when(sec == 1)
+    def _():
+        finish(SIG, 2)
+
+    for h in range(2):
+        send_z(h).wait_send()
     for h in range(2):
         finish(FAC, h)
         finish(INV, h, (DOWN,))
@@ -379,8 +438,9 @@
             pltpu.VMEM((n * t, t), low),
             pltpu.VMEM((2, 2, t, t), low),
             pltpu.VMEM((2, t, 2 * t), low),
-            dma((4, 3, n, 2)), dma((4, 3, n)), dma((n,)), dma((3, n)),
-            dma((3, n)), dma((3, n)), dma((2,)), dma((2,)), dma(()), dma(()),
+            pltpu.VMEM((2, t, t), jnp.float32),
+            dma((4, 3, n, 2)), dma((4, 3, n)), dma((2, n)), dma((3, n)),
+            dma((3, n)), dma((3, n)), dma((2,)), dma((2,)), dma((2,)), dma((2,)),
         ],
         compiler_params=pltpu.CompilerParams(
             collective_id=0, has_side_effects=True, vmem_limit_bytes=56 * 2**20

time: 217 us -> 213 us (0.982)
    pallas_call x1, Pallas kernels: 212 us -> 210 us  [fused(): pl.pallas_call(lambda *refs: kernel(n, *refs), out_shape=jax.ShapeDtypeSt...]
where the time goes in v4:
time: 213 us
  Pallas kernels  210 us (99%)
  local copies, waits for them, and re-layouts  3.16 us (1%)
    pallas_call x1, Pallas kernels, fused(): pl.pallas_call(lambda *refs: kernel(n, *refs), out_shape=jax.ShapeDtypeSt...  210 us

profile of v4, /device:TPU:1, one launch (start us, length us, event | category | flops | bytes accessed | tf_op | source)
XLA Modules:
  0.0 212.8 jit_solution(8270435452970553783)
XLA Ops:
  0.0 209.7 %shard_map.37 = f32[1,512,1024]{2,1,0:T(8,128)} custom-call(bf16[1,512,1024]{2,1,0:T(8,128)(2,1)} %refs_0_.1, bf16[1,512,1024]{2,1,0:T(8,128)(2,1)} %refs_1_.1, f32[512,1024]{1,0:T(8,128)} %refs_2_.1), custom_call_target="tpu_custom_call" | custom-call | tf_op jit(solution)/shard_map/pallas_call | solution.py:429
  209.7 3.2 %copy.5 = f32[1,512,1024]{2,1,0:T(8,128)} copy(f32[1,512,1024]{2,1,0:T(8,128)} %shard_map.37) | data formatting | bytes 4194304

commit v5 on v4

--- a/solution.py
+++ b/solution.py
@@ -77,7 +77,7 @@
     owners = (c == r // 2, c == r // 2, jnp.logical_and(c == 0, r == 1))
     picks = (r % 2, r % 2, 0)
     spans = {
-        SIG: ((0, t), (0, t // 2), (t // 2, t // 2)),
+        SIG: ((0, t), (0, t // 4), (t // 4, t - t // 4)),
         STA: ((0, t), (0, t // 4), (t // 4, t - t // 4)),
     }
 
@@ -194,21 +194,35 @@
     for h in range(2):
         sb[h, rows(r), :] = s_ref[:, cols(h)].astype(jnp.bfloat16)
 
+    for h in range(2):
+        gb[h, rows(r), :] = g_ref[0, :, cols(h)]
+        fb[h, rows(r), :] = f_ref[0, :, cols(h)]
+
+    def gather_sigma(d):
+        for p in range(2):
+            receive(SIG, p, d, lambda k: hop_sigma(p, k).start())
+
+    def start_both(a):
+        for h in range(2):
+            start_own(a, h)
+
     @pl.when(sec == 0)
     def _():
         start_own(SIG, 0)
         start_own(SIG, 1)
+        gather_sigma(1)
+        start_both(INV)
+        gather_sigma(2)
+        start_both(FAC)
+        for d in range(3, n):
+            gather_sigma(d)
 
     @pl.when(sec == 1)
     def _():
         start_own(SIG, 2)
-
-    for h in range(2):
-        gb[h, rows(r), :] = g_ref[0, :, cols(h)]
-        start_own(INV, h)
-    for h in range(2):
-        fb[h, rows(r), :] = f_ref[0, :, cols(h)]
-        start_own(FAC, h)
+        start_both(INV)
+        start_both(FAC)
+
     for a in range(3):
         share_left(a, r)
 
@@ -217,16 +231,6 @@
             @pl.when(jnp.logical_and(k > r, k < 2 * c + h))
             def _():
                 gb[h, rows(k), :] = jnp.zeros((t, t), jnp.bfloat16)
-
-    def gather_sigma(d):
-        @pl.when(sec == 0)
-        def _():
-            for p in range(2):
-                receive(SIG, p, d, lambda k: hop_sigma(p, k).start())
-
-        @pl.when(sec == 1)
-        def _():
-            receive(SIG, 2, d)
 
     def add_rows(buf, k, first=False):
         for h in range(2):
@@ -292,7 +296,10 @@
 
         if d == n - 2:
             diagonals()
-        gather_sigma(d)
+        @pl.when(sec == 1)
+        def _():
+            receive(SIG, 2, d)
+
         for h in range(2):
             receive(FAC, h, d)
         ranked(d, lambda k: share_left(FAC, k))

time: 213 us -> 209 us (0.981)
  Pallas kernels: 210 us -> 206 us
    pallas_call x1, Pallas kernels: 210 us -> 206 us  [fused(): pl.pallas_call(lambda *refs: kernel(n, *refs), out_shape=jax.ShapeDtypeSt...]
where the time goes in v5:
time: 209 us
  Pallas kernels  206 us (99%)
  local copies, waits for them, and re-layouts  3.16 us (2%)
    pallas_call x1, Pallas kernels, fused(): pl.pallas_call(lambda *refs: kernel(n, *refs), out_shape=jax.ShapeDtypeSt...  206 us

profile of v5, /device:TPU:1, one launch (start us, length us, event | category | flops | bytes accessed | tf_op | source)
XLA Modules:
  0.0 209.2 jit_solution(5468965835766925928)
XLA Ops:
  0.0 206.0 %shard_map.37 = f32[1,512,1024]{2,1,0:T(8,128)} custom-call(bf16[1,512,1024]{2,1,0:T(8,128)(2,1)} %refs_0_.1, bf16[1,512,1024]{2,1,0:T(8,128)(2,1)} %refs_1_.1, f32[512,1024]{1,0:T(8,128)} %refs_2_.1), custom_call_target="tpu_custom_call" | custom-call | tf_op jit(solution)/shard_map/pallas_call | solution.py:436
  206.0 3.2 %copy.5 = f32[1,512,1024]{2,1,0:T(8,128)} copy(f32[1,512,1024]{2,1,0:T(8,128)} %shard_map.37) | data formatting | bytes 4194304

commit v6 on v5

--- a/solution.py
+++ b/solution.py
@@ -300,6 +300,13 @@
         def _():
             receive(SIG, 2, d)
 
+        if d == n - 1:
+            @pl.when(sec == 0)
+            def _():
+                for p in (1, 0):
+                    hop_state(p, r).wait_recv()
+                    start_own(STA, p)
+
         for h in range(2):
             receive(FAC, h, d)
         ranked(d, lambda k: share_left(FAC, k))
@@ -355,9 +362,9 @@
             if h == 1:
                 hop_state(1, r).start()
                 start_own(STA, 2)
-                hop_state(2, r).start()
             else:
                 hop_state(0, r).start()
+                hop_state(2, r).start()
 
         products(onward)
         for d in range(1, n):
@@ -374,9 +381,6 @@
 
     @pl.when(sec == 0)
     def _():
-        for p in (1, 0):
-            hop_state(p, r).wait_recv()
-            start_own(STA, p)
         for d in range(1, n):
             for p in (1, 0):
                 receive(STA, p, d)

time: 209 us -> 209 us (level)
  no operation moved by 1% of the time
where the time goes in v6:
time: 209 us
  Pallas kernels  206 us (99%)
  local copies, waits for them, and re-layouts  3.16 us (2%)
    pallas_call x1, Pallas kernels, fused(): pl.pallas_call(lambda *refs: kernel(n, *refs), out_shape=jax.ShapeDtypeSt...  206 us

profile of v6, /device:TPU:1, one launch (start us, length us, event | category | flops | bytes accessed | tf_op | source)
XLA Modules:
  0.0 209.2 jit_solution(11738545050490632605)
XLA Ops:
  0.0 206.0 %shard_map.37 = f32[1,512,1024]{2,1,0:T(8,128)} custom-call(bf16[1,512,1024]{2,1,0:T(8,128)(2,1)} %refs_0_.1, bf16[1,512,1024]{2,1,0:T(8,128)(2,1)} %refs_1_.1, f32[512,1024]{1,0:T(8,128)} %refs_2_.1), custom_call_target="tpu_custom_call" | custom-call | tf_op jit(solution)/shard_map/pallas_call | solution.py:440
  206.0 3.2 %copy.5 = f32[1,512,1024]{2,1,0:T(8,128)} copy(f32[1,512,1024]{2,1,0:T(8,128)} %shard_map.37) | data formatting | bytes 4194304
